TPU v7x, 32 devices: a whole 2x2x4 slice. The times are simulated.
32 devices in a mesh: groups: 2 (over y), seq: 4 (over z), tensor: 2 (over x), sub: 2 (over core).
Axes of the slice: x: 2, y: 2, z: 4, core: 2. Of those that a mesh axis runs over, the one named last changes fastest.
Arguments:
- activations: bfloat16 [4096, 4096], P(('groups', 'seq'), ('tensor', 'sub')), parts along dimension 0, may hold values from -18 to 18
- conv_weight: bfloat16 [512, 4096], P(None, ('tensor', 'sub')), may hold values from -0.25 to 0.25
- query_weight: bfloat16 [4096, 2048], P('seq', ('tensor', 'sub')), may hold values from -0.09375 to 0.09375
- key_weight: bfloat16 [4096, 2048], P('seq', ('tensor', 'sub')), may hold values from -0.09375 to 0.09375
- value_weight: bfloat16 [4096, 2048], P('seq', ('tensor', 'sub')), may hold values from -0.09375 to 0.09375
- segment_for_slot: int32 [16], P('groups'), parts along dimension 0, may hold values from 0 to 7, each once
- book_length: int32 [2], P('groups'), parts along dimension 0, may hold values from 1024 to 2048
Outputs:
- context: bfloat16 [4096, 2048], P(('groups', 'seq'), ('tensor', 'sub')), parts along dimension 0
There are 2 independent parts, one for each index of `groups`. A program takes and returns all parts, laid end to end along the dimension named above; an argument that names none is the same for every part. Nothing has to cross between parts.
Inputs may be any that keep to these rules, and one draw needn't show every extreme that they name: `segment_for_slot`: each segment appears in exactly one slot.
All inputs are finite; a program needn't handle non-finite values.
Results may differ from a plain program's by a relative error of at most 0.012.
The roundings to bfloat16 on the way count: a program that leaves them out, or rounds other values in their place, can miss the bound.
Values may be sent and summed in bfloat16 or wider, within the bound.
No kernel may reach another device: no remote copies, remote signals or barrier semaphores. Data moves between devices by JAX's collectives and lax.ppermute only.
A program may use at most 64 MiB of HBM per device.

v0:
```python
import jax
import jax.numpy as jnp
from jax import lax
from jax.sharding import PartitionSpec as P

HD = 128
CG = 128
RATE = 4
SLOTS = 2
SEG = 256
MEM = 64


def compress_rows(local_rows, conv_local):
    count_rows, channels = local_rows.shape
    groups = channels // CG
    shaped = local_rows.reshape(count_rows // RATE, RATE, groups, CG)
    kernel = conv_local.reshape(RATE, CG, groups, CG)
    mixed_out = jnp.einsum("mtgc,tcgo->mgo", shaped, kernel, preferred_element_type=jnp.float32)
    return mixed_out.reshape(count_rows // RATE, channels).astype(jnp.bfloat16)


def add_product(source, weight_rows):
    return jnp.dot(source, weight_rows, preferred_element_type=jnp.float32)


def local_attention(queries, keys_here, values_here):
    total_rows, head_count, head_dim = queries.shape
    slot_count = total_rows // SEG
    shaped_q = queries.reshape(slot_count, SEG, head_count, head_dim)
    shaped_k = keys_here.reshape(slot_count, SEG, head_count, head_dim)
    shaped_v = values_here.reshape(slot_count, SEG, head_count, head_dim)
    scores = jnp.einsum(
        "asnd,atnd->asnt", shaped_q, shaped_k, preferred_element_type=jnp.float32
    ) * HD ** (-0.5)
    causal = jnp.arange(SEG, dtype=jnp.int32)[:, None] >= jnp.arange(SEG, dtype=jnp.int32)[None, :]
    scores = jnp.where(causal[None, :, None, :], scores, -jnp.inf)
    row_best = jnp.max(scores, axis=3)
    weights = jnp.exp(scores - row_best[..., None])
    denominator = jnp.sum(weights, axis=3)
    weighted_numerator = jnp.einsum(
        "asnt,atnd->asnd",
        weights.astype(jnp.bfloat16),
        shaped_v,
        preferred_element_type=jnp.float32,
    )
    return (
        row_best.reshape(total_rows, head_count),
        denominator.reshape(total_rows, head_count),
        weighted_numerator.reshape(total_rows, head_count, head_dim),
    )


def memory_step(state, pieces, queries, row_segment, segment_for_slot):
    keys_in, values_in = pieces
    count_keys = keys_in.shape[0]
    total_rows, head_count, head_dim = queries.shape
    key_slot = jnp.arange(count_keys, dtype=jnp.int32) // MEM
    slot_ids = jnp.arange(segment_for_slot.shape[0], dtype=jnp.int32)
    key_segment = jnp.sum(
        jnp.where(key_slot[:, None] == slot_ids[None, :], segment_for_slot[None, :], 0), axis=1
    )
    row_best, denominator, weighted_numerator = state
    shaped_keys = keys_in.reshape(count_keys, head_count, head_dim)
    shaped_values = values_in.reshape(count_keys, head_count, head_dim)
    scores = jnp.einsum(
        "rnd,knd->rnk", queries, shaped_keys, preferred_element_type=jnp.float32
    ) * HD ** (-0.5)
    allowed = key_segment[None, None, :] < row_segment[:, None, None]
    scores = jnp.where(allowed, scores, -jnp.inf)
    new_best = jnp.maximum(row_best, jnp.max(scores, axis=2))
    weights = jnp.exp(scores - new_best[:, :, None])
    factor = jnp.exp(row_best - new_best)
    denominator = denominator * factor + jnp.sum(weights, axis=2)
    weighted_numerator = weighted_numerator * factor[:, :, None] + jnp.einsum(
        "rnk,knd->rnd",
        weights.astype(jnp.bfloat16),
        shaped_values,
        preferred_element_type=jnp.float32,
    )
    return (new_best, denominator, weighted_numerator)


def on_device(
    activations, conv_weight, query_weight, key_weight, value_weight, segment_for_slot, book_length
):
    compressed_local = compress_rows(activations, conv_weight)
    full_rows, full_compressed = (
        lax.all_gather(activations, ("tensor", "sub"), axis=1, tiled=True),
        lax.all_gather(compressed_local, ("tensor", "sub"), axis=1, tiled=True),
    )
    total_rows = full_rows.shape[0]
    local_width = query_weight.shape[1]
    head_count = local_width // HD
    shard_index = lax.axis_index("seq")
    my_segments = lax.dynamic_slice_in_dim(segment_for_slot, shard_index * SLOTS, SLOTS, 0)
    row_segment = jnp.repeat(my_segments, SEG, total_repeat_length=total_rows)
    query_rows = lax.all_gather(query_weight, "seq", axis=0, tiled=True)
    key_matrix_rows = lax.all_gather(key_weight, "seq", axis=0, tiled=True)
    value_rows = lax.all_gather(value_weight, "seq", axis=0, tiled=True)
    queries = add_product(full_rows, query_rows).astype(jnp.bfloat16)
    keys_here = add_product(full_rows, key_matrix_rows).astype(jnp.bfloat16)
    values_here = add_product(full_rows, value_rows).astype(jnp.bfloat16)
    keys_mem = add_product(full_compressed, key_matrix_rows).astype(jnp.bfloat16)
    values_mem = add_product(full_compressed, value_rows).astype(jnp.bfloat16)
    shaped_q = queries.reshape(total_rows, head_count, HD)
    state = local_attention(
        shaped_q,
        keys_here.reshape(total_rows, head_count, HD),
        values_here.reshape(total_rows, head_count, HD),
    )
    state = memory_step(
        state,
        (
            lax.all_gather(keys_mem, "seq", axis=0, tiled=True),
            lax.all_gather(values_mem, "seq", axis=0, tiled=True),
        ),
        shaped_q,
        row_segment,
        segment_for_slot,
    )
    row_best, denominator, weighted_numerator = state
    result = (weighted_numerator / denominator[:, :, None]).reshape(total_rows, local_width)
    position = row_segment * SEG + jnp.arange(total_rows, dtype=jnp.int32) % SEG
    result = jnp.where((position < book_length[0])[:, None], result, 0.0)
    return result.astype(jnp.bfloat16)


def solution(mesh):
    placed = (
        P(("groups", "seq"), ("tensor", "sub")),
        P(None, ("tensor", "sub")),
        P("seq", ("tensor", "sub")),
        P("seq", ("tensor", "sub")),
        P("seq", ("tensor", "sub")),
        P("groups"),
        P("groups"),
    )
    return jax.shard_map(
        on_device,
        mesh=mesh,
        in_specs=placed,
        out_specs=P(("groups", "seq"), ("tensor", "sub")),
        check_vma=False,
    )
```

profile of v0, /device:TPU:0, one launch (start us, length us, event | category | flops | bytes accessed | tf_op | source)
XLA Modules:
  0.0 350.5 jit_solution(3054702752094949203)
XLA Ops:
  6.5 0.7 all-gather.6.cloned.1.call-update
  7.3 0.7 all-gather.10.cloned.1.call-update
  8.1 0.7 all-gather.12.cloned.1.call-update
  8.8 1.5 copy.64
  10.6 1.7 fusion.17
  13.6 0.6 fusion.41
  14.3 1.3 fusion.32
  15.6 1.3 broadcast_select_fusion
  17.1 29.0 %all-gather.6.cloned.1.call-done = bf16[512,4096]{1,0:T(8,128)(2,1)} async-done(((bf16[512,1024]{1,0:T(8,128)(2,1)}), bf16[512,4096]{1,0:T(8,128)(2,1)}) %all-gather.6.cloned.1.call-update) | async-done | bytes 4194320 | tf_op jit(solution)/shard_map/all_gather | solution.py:89
  46.1 82.4 %all-gather.10.cloned.1.call-done = bf16[4096,512]{1,0:T(8,128)(2,1)} async-done(((bf16[1024,512]{1,0:T(8,128)(2,1)}), bf16[4096,512]{1,0:T(8,128)(2,1)}) %all-gather.10.cloned.1.call-update) | async-done | bytes 4194320 | tf_op jit(solution)/shard_map/all_gather | solution.py:99
  128.5 5.8 %convolution_convert_fusion.1 = bf16[512,512]{1,0:T(8,128)(2,1)S(1)} fusion(bf16[512,4096]{1,0:T(8,128)(2,1)} %all-gather.6.cloned.1.call-done, bf16[4096,512]{1,0:T(8,128)(2,1)} %all-gather.10.cloned.1.call-done), kind=kOutput, calls=%fused_computation.18 | convolution fusion | flops 2147745792 | bytes 8912896 | tf_op jit(solution)/shard_map/dot_general | solution.py:24
  134.4 75.0 %all-gather.12.cloned.1.call-done = bf16[4096,512]{1,0:T(8,128)(2,1)} async-done(((bf16[1024,512]{1,0:T(8,128)(2,1)}), bf16[4096,512]{1,0:T(8,128)(2,1)}) %all-gather.12.cloned.1.call-update) | async-done | bytes 4194320 | tf_op jit(solution)/shard_map/all_gather | solution.py:98
  209.4 5.8 %convolution_convert_fusion = bf16[512,512]{0,1:T(8,128)(2,1)S(1)} fusion(bf16[512,4096]{1,0:T(8,128)(2,1)} %all-gather.6.cloned.1.call-done, bf16[4096,512]{1,0:T(8,128)(2,1)} %all-gather.12.cloned.1.call-done), kind=kOutput, calls=%fused_computation.17 | convolution fusion | flops 2147745792 | bytes 8912896 | tf_op jit(solution)/shard_map/dot_general | solution.py:24
  215.4 10.7 %all-gather.14.cloned.1.call-done = bf16[128,4096]{0,1:T(8,128)(2,1)} async-done(((bf16[128,1024]{0,1:T(8,128)(2,1)}), bf16[128,4096]{0,1:T(8,128)(2,1)}) %all-gather.14.cloned.1.call-update) | async-done | bytes 1048592 | tf_op jit(solution)/shard_map/all_gather | solution.py:90
  226.1 3.3 convolution_convert_fusion.4
  229.4 21.4 %all_gather.26 = bf16[512,512]{1,0:T(8,128)(2,1)} all-gather(bf16[128,512]{1,0:T(8,128)(2,1)S(1)} %convolution_convert_fusion.4), channel_id=1, replica_groups=mesh['groups'=2,'seq'=4,'tensor'=2,'sub'=2] {'seq'}, dimensions={0}, use_global_device_ids=true | all-gather | bytes 655360 | tf_op jit(solution)/shard_map/all_gather | solution.py:115
  250.8 61.4 %all-gather.8.cloned.1.call-done = bf16[4096,512]{1,0:T(8,128)(2,1)} async-done(((bf16[1024,512]{1,0:T(8,128)(2,1)}), bf16[4096,512]{1,0:T(8,128)(2,1)}) %all-gather.8.cloned.1.call-update) | async-done | bytes 4194320 | tf_op jit(solution)/shard_map/all_gather | solution.py:100
  312.2 5.8 %convolution_convert_fusion.2 = bf16[512,512]{1,0:T(8,128)(2,1)S(1)} fusion(bf16[512,4096]{1,0:T(8,128)(2,1)} %all-gather.6.cloned.1.call-done, bf16[4096,512]{1,0:T(8,128)(2,1)} %all-gather.8.cloned.1.call-done), kind=kOutput, calls=%fused_computation.19 | convolution fusion | flops 2147745792 | bytes 8912896 | tf_op jit(solution)/shard_map/dot_general | solution.py:24
  320.1 3.0 convolution_convert_fusion.3
  323.1 15.2 %all_gather.27 = bf16[512,512]{1,0:T(8,128)(2,1)S(1)} all-gather(bf16[128,512]{1,0:T(8,128)(2,1)S(1)} %convolution_convert_fusion.3), channel_id=1, replica_groups=mesh['groups'=2,'seq'=4,'tensor'=2,'sub'=2] {'seq'}, dimensions={0}, use_global_device_ids=true | all-gather | bytes 655360 | tf_op jit(solution)/shard_map/all_gather | solution.py:116
  338.6 1.9 fusion.2
  340.5 0.9 fusion
  341.4 1.4 fusion.22
  343.0 1.0 select_convert_fusion
  (37 shorter events, 4.2 us)
Async XLA Ops:
  6.5 3.8 %copy-start = (bf16[512,1024]{1,0:T(8,128)(2,1)S(1)}, bf16[512,1024]{1,0:T(8,128)(2,1)}, u32[]{:S(2)}) copy-start(bf16[512,1024]{1,0:T(8,128)(2,1)} %param.9) | copy-start | bytes 3145732
  6.5 39.6 %all-gather.6.cloned.1.call-start = ((), (), s32[]{:S(2)}) async-start(), calls=%async_computation | async-start | bytes 5242880 | tf_op jit(solution)/shard_map/all_gather | solution.py:89
  7.3 121.2 %all-gather.10.cloned.1.call-start = ((), (), s32[]{:S(2)}) async-start(), calls=%async_computation.2 | async-start | bytes 5242880 | tf_op jit(solution)/shard_map/all_gather | solution.py:99
  8.0 201.4 %all-gather.12.cloned.1.call-start = ((), (), s32[]{:S(2)}) async-start(), calls=%async_computation.3 | async-start | bytes 5242880 | tf_op jit(solution)/shard_map/all_gather | solution.py:98
  8.7 217.4 %all-gather.14.cloned.1.call-start = ((), (), s32[]{:S(2)}) async-start(), calls=%async_computation.4 | async-start | bytes 1310720 | tf_op jit(solution)/shard_map/all_gather | solution.py:90
  8.8 4.8 %copy-start.5 = (s32[8]{0:T(128)S(1)}, s32[8]{0:T(128)}, u32[]{:S(2)}) copy-start(s32[8]{0:T(128)} %param.14) | copy-start | bytes 100
  8.8 5.5 %copy-start.4 = (pred[512]{0:T(512)(128)(4,1)S(1)}, pred[512]{0:T(512)(128)(4,1)}, u32[]{:S(2)}) copy-start(pred[512]{0:T(512)(128)(4,1)} %constant.157) | copy-start | bytes 1540
  12.3 299.9 %all-gather.8.cloned.1.call-start = ((), (), s32[]{:S(2)}) async-start(), calls=%async_computation.1 | async-start | bytes 5242880 | tf_op jit(solution)/shard_map/all_gather | solution.py:100
  215.2 96.9 %copy-start.3 = (bf16[512,512]{0,1:T(8,128)(2,1)}, bf16[512,512]{0,1:T(8,128)(2,1)S(1)}, u32[]{:S(2)}) copy-start(bf16[512,512]{0,1:T(8,128)(2,1)S(1)} %convolution_convert_fusion) | copy-start | bytes 1572868
  318.9 1.2 copy-start.1
  320.1 18.4 %copy-start.2 = (bf16[512,512]{1,0:T(8,128)(2,1)S(1)}, bf16[512,512]{1,0:T(8,128)(2,1)}, u32[]{:S(2)}) copy-start(bf16[512,512]{1,0:T(8,128)(2,1)} %all_gather.26) | copy-start | bytes 1572868
Sparse Core Ops, SparseCore 0:
  8.9 37.1 all-gather.5
  47.7 80.7 all-gather.9
  130.1 79.2 all-gather.11
  210.8 15.2 all-gather.13
  227.5 84.6 all-gather.7
where the time goes:
time: 351 us
  waiting for transfers between devices  261 us (74%)
  blocking collectives  36.6 us (10%)
  matrix products  29.6 us (8%)
  between operations  14 us (4%)
  other arithmetic  5.11 us (1%)
  local copies, waits for them, and re-layouts  3.95 us (1%)
    all_gather x1, waiting for transfers between devices, on_device(): key_matrix_rows = lax.all_gather(key_weight, 'seq', axis=0, tiled=True)  82.4 us
    all_gather x1, waiting for transfers between devices, on_device(): query_rows = lax.all_gather(query_weight, 'seq', axis=0, tiled=True)  75 us
    all_gather x1, waiting for transfers between devices, on_device(): value_rows = lax.all_gather(value_weight, 'seq', axis=0, tiled=True)  61.4 us
    all_gather x1, waiting for transfers between devices, on_device(): lax.all_gather(activations, ('tensor', 'sub'), axis=1, tiled=True)  29 us
    dot_general x5, matrix products, add_product(): return jnp.dot(source, weight_rows, preferred_element_type=jnp.float32)  23.6 us
    all_gather x1, blocking collectives, on_device(): lax.all_gather(keys_mem, 'seq', axis=0, tiled=True)  21.4 us
    all_gather x1, blocking collectives, on_device(): lax.all_gather(values_mem, 'seq', axis=0, tiled=True)  15.2 us
    all_gather x1, waiting for transfers between devices, on_device(): lax.all_gather(compressed_local, ('tensor', 'sub'), axis=1, tiled=True)  10.7 us
  transfers between devices with their start and end apart: 5, of which 5 were waited for; matrix products, arithmetic and copies ran while one was open for 6% of the time, Pallas kernels for 0%

commit v1 on v0

--- a/solution.py
+++ b/solution.py
@@ -96,7 +96,26 @@
     my_segments = lax.dynamic_slice_in_dim(segment_for_slot, shard_index * SLOTS, SLOTS, 0)
     row_segment = jnp.repeat(my_segments, SEG, total_repeat_length=total_rows)
     query_rows = lax.all_gather(query_weight, "seq", axis=0, tiled=True)
-    key_matrix_rows = lax.all_gather(key_weight, "seq", axis=0, tiled=True)
+    size, index, rows = (lax.axis_size("seq"), lax.axis_index("seq"), key_weight.shape[0])
+    forward = [(i, (i + 1) % size) for i in range(size)]
+    left = [(i, (i - 1) % size) for i in range(size)]
+    filled = jnp.zeros(
+        (*key_weight.shape[:0], size * rows, *key_weight.shape[0 + 1 :]), key_weight.dtype
+    )
+    filled = lax.dynamic_update_slice_in_dim(filled, key_weight, index * rows, axis=0)
+    from_left = from_right = key_weight
+    halfway = size // 2
+    for hop in range(1, halfway + 1):
+        from_left = lax.ppermute(from_left, "seq", forward)
+        filled = lax.dynamic_update_slice_in_dim(
+            filled, from_left, (index - hop) % size * rows, axis=0
+        )
+        if hop < size - halfway:
+            from_right = lax.ppermute(from_right, "seq", left)
+            filled = lax.dynamic_update_slice_in_dim(
+                filled, from_right, (index + hop) % size * rows, axis=0
+            )
+    key_matrix_rows = filled
     value_rows = lax.all_gather(value_weight, "seq", axis=0, tiled=True)
     queries = add_product(full_rows, query_rows).astype(jnp.bfloat16)
     keys_here = add_product(full_rows, key_matrix_rows).astype(jnp.bfloat16)

time: 351 us -> 284 us (0.81)
  waiting for transfers between devices: 261 us -> 171 us
  blocking collectives: 36.6 us -> 47.6 us
  local copies, waits for them, and re-layouts: 3.95 us -> 11.8 us
  starting transfers between devices: 0.16 us -> 5.29 us
    all_gather x1 -> x0, waiting for transfers between devices: 82.4 us -> none  [on_device(): key_matrix_rows = lax.all_gather(key_weight, 'seq', axis=0, tiled=True)]
    ppermute x0 -> x3, waiting for transfers between devices: none -> 65.9 us  [the longest x2 49.1 us: on_device(): from_left = lax.ppermute(from_left, 'seq', forward)]
    all_gather x1, waiting for transfers between devices: 75 us -> 27.4 us  [on_device(): query_rows = lax.all_gather(query_weight, 'seq', axis=0, tiled=True)]
    all_gather x1, waiting for transfers between devices: 29 us -> 0.01 us  [on_device(): lax.all_gather(activations, ('tensor', 'sub'), axis=1, tiled=True)]
    all_gather x1, waiting for transfers between devices: 61.4 us -> 75.4 us  [on_device(): value_rows = lax.all_gather(value_weight, 'seq', axis=0, tiled=True)]
    all_gather x1, waiting for transfers between devices: 10.7 us -> 0.01 us  [on_device(): lax.all_gather(compressed_local, ('tensor', 'sub'), axis=1, tiled=True)]
    all_gather x1, blocking collectives: 21.4 us -> 31.2 us  [on_device(): lax.all_gather(keys_mem, 'seq', axis=0, tiled=True)]
    ppermute x0 -> x3, starting transfers between devices: none -> 5.17 us  [the longest x2 3.08 us: on_device(): from_left = lax.ppermute(from_left, 'seq', forward)]
  transfers between devices with their start and end apart: 5 -> 7, of which waited for: 5 -> 5; matrix products, arithmetic and copies ran while one was open for 6% -> 9% of each run, Pallas kernels for 0% -> 0%
where the time goes in v1:
time: 284 us
  waiting for transfers between devices  171 us (60%)
  blocking collectives  47.6 us (17%)
  matrix products  29.7 us (10%)
  between operations  14 us (5%)
  local copies, waits for them, and re-layouts  11.8 us (4%)
  starting transfers between devices  5.29 us (2%)
  other arithmetic  5.15 us (2%)
    all_gather x1, waiting for transfers between devices, on_device(): value_rows = lax.all_gather(value_weight, 'seq', axis=0, tiled=True)  75.4 us
    ppermute x2, waiting for transfers between devices, on_device(): from_left = lax.ppermute(from_left, 'seq', forward)  49.1 us
    all_gather x1, blocking collectives, on_device(): lax.all_gather(keys_mem, 'seq', axis=0, tiled=True)  31.2 us
    all_gather x1, waiting for transfers between devices, on_device(): query_rows = lax.all_gather(query_weight, 'seq', axis=0, tiled=True)  27.4 us
    dot_general x5, matrix products, add_product(): return jnp.dot(source, weight_rows, preferred_element_type=jnp.float32)  23.8 us
    ppermute x1, waiting for transfers between devices, on_device(): from_right = lax.ppermute(from_right, 'seq', left)  16.7 us
    all_gather x1, blocking collectives, on_device(): lax.all_gather(values_mem, 'seq', axis=0, tiled=True)  16.4 us
  transfers between devices with their start and end apart: 7, of which 5 were waited for; matrix products, arithmetic and copies ran while one was open for 9% of the time, Pallas kernels for 0%

profile of v1, /device:TPU:0, one launch (start us, length us, event | category | flops | bytes accessed | tf_op | source)
XLA Modules:
  0.0 284.1 jit_solution(3277889132892866081)
XLA Ops:
  6.5 1.5 copy.64
  8.0 1.6 copy.65
  9.6 1.7 fusion.18
  13.4 3.1 %collective-permute-start = (bf16[1024,512]{1,0:T(8,128)(2,1)S(1)}, bf16[1024,512]{1,0:T(8,128)(2,1)S(1)}, u32[]{:S(2)}, u32[]{:S(2)}) collective-permute-start(bf16[1024,512]{1,0:T(8,128)(2,1)S(1)} %copy-done.1), channel_id=1, source_target_pairs={{0,4},{4,8},{8,12},{12,0},{1,5},{5,9},{9,13},{13,1},{2,6},{6,10},{... | collective-permute-start | bytes 3145736 | tf_op jit(solution)/shard_map/ppermute | solution.py:109
  16.5 2.1 collective-permute-start.1
  18.6 2.2 broadcast_in_dim.75
  20.8 1.1 constant_dynamic-update-slice_fusion.3
  22.8 19.8 %collective-permute-done = bf16[1024,512]{1,0:T(8,128)(2,1)S(1)} collective-permute-done((bf16[1024,512]{1,0:T(8,128)(2,1)S(1)}, bf16[1024,512]{1,0:T(8,128)(2,1)S(1)}, u32[]{:S(2)}, u32[]{:S(2)}) %collective-permute-start) | collective-permute-done | bytes 1048608 | tf_op jit(solution)/shard_map/ppermute | solution.py:109
  43.2 1.3 fusion.33
  44.5 1.3 broadcast_select_fusion
  46.0 1.0 constant_dynamic-update-slice_fusion.2
  47.1 16.7 %collective-permute-done.1 = bf16[1024,512]{1,0:T(8,128)(2,1)S(1)} collective-permute-done((bf16[1024,512]{1,0:T(8,128)(2,1)S(1)}, bf16[1024,512]{1,0:T(8,128)(2,1)S(1)}, u32[]{:S(2)}, u32[]{:S(2)}) %collective-permute-start.1) | collective-permute-done | bytes 1048608 | tf_op jit(solution)/shard_map/ppermute | solution.py:114
  64.9 29.4 %collective-permute-done.2 = bf16[1024,512]{1,0:T(8,128)(2,1)S(1)} collective-permute-done((bf16[1024,512]{1,0:T(8,128)(2,1)S(1)}, bf16[1024,512]{1,0:T(8,128)(2,1)S(1)}, u32[]{:S(2)}, u32[]{:S(2)}) %collective-permute-start.2) | collective-permute-done | bytes 1048608 | tf_op jit(solution)/shard_map/ppermute | solution.py:109
  95.3 3.3 %convolution_convert_fusion.4 = bf16[128,512]{1,0:T(8,128)(2,1)S(1)} fusion(bf16[128,4096]{0,1:T(8,128)(2,1)} %all-gather.11.cloned.1.call-done, bf16[4096,512]{1,0:T(8,128)(2,1)} %constant_dynamic-update-slice_fusion), kind=kOutput, calls=%fused_computation.24 | convolution fusion | flops 536936448 | bytes 5373952 | tf_op jit(solution)/shard_map/dot_general | solution.py:24
  98.6 31.2 %all_gather.22 = bf16[512,512]{1,0:T(8,128)(2,1)} all-gather(bf16[128,512]{1,0:T(8,128)(2,1)S(1)} %convolution_convert_fusion.4), channel_id=1, replica_groups=mesh['groups'=2,'seq'=4,'tensor'=2,'sub'=2] {'seq'}, dimensions={0}, use_global_device_ids=true | all-gather | bytes 655360 | tf_op jit(solution)/shard_map/all_gather | solution.py:134
  129.8 5.9 %fusion.17 = bf16[512,512]{0,1:T(8,128)(2,1)S(1)} fusion(bf16[4096,512]{1,0:T(8,128)(2,1)} %constant_dynamic-update-slice_fusion, bf16[512,4096]{1,0:T(8,128)(2,1)} %all-gather.5.cloned.1.call-done), kind=kOutput, calls=%fused_computation.21 | convolution fusion | flops 2147745792 | bytes 8912896 | tf_op jit(solution)/shard_map/dot_general | solution.py:24
  135.8 27.4 %all-gather.9.cloned.1.call-done = bf16[4096,512]{1,0:T(8,128)(2,1)} async-done(((bf16[1024,512]{1,0:T(8,128)(2,1)}), bf16[4096,512]{1,0:T(8,128)(2,1)}) %all-gather.9.cloned.1.call-update) | async-done | bytes 4194320 | tf_op jit(solution)/shard_map/all_gather | solution.py:98
  163.2 5.8 %convolution_convert_fusion = bf16[512,512]{0,1:T(8,128)(2,1)S(1)} fusion(bf16[512,4096]{1,0:T(8,128)(2,1)} %all-gather.5.cloned.1.call-done, bf16[4096,512]{1,0:T(8,128)(2,1)} %all-gather.9.cloned.1.call-done), kind=kOutput, calls=%fused_computation.17 | convolution fusion | flops 2147745792 | bytes 8912896 | tf_op jit(solution)/shard_map/dot_general | solution.py:24
  169.1 75.4 %all-gather.7.cloned.1.call-done = bf16[4096,512]{1,0:T(8,128)(2,1)} async-done(((bf16[1024,512]{1,0:T(8,128)(2,1)}), bf16[4096,512]{1,0:T(8,128)(2,1)}) %all-gather.7.cloned.1.call-update) | async-done | bytes 4194320 | tf_op jit(solution)/shard_map/all_gather | solution.py:119
  244.5 5.8 %convolution_convert_fusion.2 = bf16[512,512]{1,0:T(8,128)(2,1)S(1)} fusion(bf16[512,4096]{1,0:T(8,128)(2,1)} %all-gather.5.cloned.1.call-done, bf16[4096,512]{1,0:T(8,128)(2,1)} %all-gather.7.cloned.1.call-done), kind=kOutput, calls=%fused_computation.19 | convolution fusion | flops 2147745792 | bytes 8912896 | tf_op jit(solution)/shard_map/dot_general | solution.py:24
  252.5 3.0 %convolution_convert_fusion.3 = bf16[128,512]{1,0:T(8,128)(2,1)S(1)} fusion(bf16[128,4096]{0,1:T(8,128)(2,1)S(1)} %copy-done, bf16[4096,512]{1,0:T(8,128)(2,1)} %all-gather.7.cloned.1.call-done), kind=kOutput, calls=%fused_computation.23 | convolution fusion | flops 536936448 | bytes 5373952 | tf_op jit(solution)/shard_map/dot_general | solution.py:24
  255.5 16.4 %all_gather.23 = bf16[512,512]{1,0:T(8,128)(2,1)S(1)} all-gather(bf16[128,512]{1,0:T(8,128)(2,1)S(1)} %convolution_convert_fusion.3), channel_id=1, replica_groups=mesh['groups'=2,'seq'=4,'tensor'=2,'sub'=2] {'seq'}, dimensions={0}, use_global_device_ids=true | all-gather | bytes 655360 | tf_op jit(solution)/shard_map/all_gather | solution.py:135
  272.1 1.9 fusion.2
  274.9 1.4 fusion.23
  (45 shorter events, 10.0 us)
Async XLA Ops:
  6.5 88.7 %all-gather.11.cloned.1.call-start = ((), (), s32[]{:S(2)}) async-start(), calls=%async_computation.3 | async-start | bytes 1310720 | tf_op jit(solution)/shard_map/all_gather | solution.py:90
  8.0 5.4 %copy-start.1 = (bf16[1024,512]{1,0:T(8,128)(2,1)S(1)}, bf16[1024,512]{1,0:T(8,128)(2,1)}, u32[]{:S(2)}) copy-start(bf16[1024,512]{1,0:T(8,128)(2,1)} %param.12) | copy-start | bytes 3145732
  11.3 118.4 %all-gather.5.cloned.1.call-start = ((), (), s32[]{:S(2)}) async-start(), calls=%async_computation | async-start | bytes 5242880 | tf_op jit(solution)/shard_map/all_gather | solution.py:89
  12.1 9.8 %copy-start.5 = (s32[8]{0:T(128)S(1)}, s32[8]{0:T(128)}, u32[]{:S(2)}) copy-start(s32[8]{0:T(128)} %param.14) | copy-start | bytes 100
  12.1 31.1 %copy-start.4 = (pred[512]{0:T(512)(128)(4,1)S(1)}, pred[512]{0:T(512)(128)(4,1)}, u32[]{:S(2)}) copy-start(pred[512]{0:T(512)(128)(4,1)} %constant.187) | copy-start | bytes 1540
  12.1 151.1 %all-gather.9.cloned.1.call-start = ((), (), s32[]{:S(2)}) async-start(), calls=%async_computation.2 | async-start | bytes 5242880 | tf_op jit(solution)/shard_map/all_gather | solution.py:98
  12.8 231.7 %all-gather.7.cloned.1.call-start = ((), (), s32[]{:S(2)}) async-start(), calls=%async_computation.1 | async-start | bytes 5242880 | tf_op jit(solution)/shard_map/all_gather | solution.py:119
  13.4 29.1 %collective-permute-start = (bf16[1024,512]{1,0:T(8,128)(2,1)S(1)}, bf16[1024,512]{1,0:T(8,128)(2,1)S(1)}, u32[]{:S(2)}, u32[]{:S(2)}) collective-permute-start(bf16[1024,512]{1,0:T(8,128)(2,1)S(1)} %copy-done.1), channel_id=1, source_target_pairs={{0,4},{4,8},{8,12},{12,0},{1,5},{5,9},{9,13},{13,1},{2,6},{6,10},{... | collective-permute-start | bytes 3145736 | tf_op jit(solution)/shard_map/ppermute | solution.py:109
  16.5 47.3 %collective-permute-start.1 = (bf16[1024,512]{1,0:T(8,128)(2,1)S(1)}, bf16[1024,512]{1,0:T(8,128)(2,1)S(1)}, u32[]{:S(2)}, u32[]{:S(2)}) collective-permute-start(bf16[1024,512]{1,0:T(8,128)(2,1)S(1)} %copy-done.1), channel_id=1, source_target_pairs={{0,12},{4,0},{8,4},{12,8},{1,13},{5,1},{9,5},{13,9},{2,14},{6,2},{... | collective-permute-start | bytes 3145736 | tf_op jit(solution)/shard_map/ppermute | solution.py:114
  42.6 51.7 %collective-permute-start.2 = (bf16[1024,512]{1,0:T(8,128)(2,1)S(1)}, bf16[1024,512]{1,0:T(8,128)(2,1)S(1)}, u32[]{:S(2)}, u32[]{:S(2)}) collective-permute-start(bf16[1024,512]{1,0:T(8,128)(2,1)S(1)} %collective-permute-done), channel_id=1, source_target_pairs={{0,4},{4,8},{8,12},{12,0},{1,5},{5,9},{9,13},{13,1},{2,6},{6,10},{... | collective-permute-start | bytes 3145736 | tf_op jit(solution)/shard_map/ppermute | solution.py:109
  169.0 75.5 %copy-start.3 = (bf16[512,512]{0,1:T(8,128)(2,1)}, bf16[512,512]{0,1:T(8,128)(2,1)S(1)}, u32[]{:S(2)}) copy-start(bf16[512,512]{0,1:T(8,128)(2,1)S(1)} %convolution_convert_fusion) | copy-start | bytes 1572868
  251.3 1.2 copy-start
  252.5 19.6 %copy-start.2 = (bf16[512,512]{1,0:T(8,128)(2,1)S(1)}, bf16[512,512]{1,0:T(8,128)(2,1)}, u32[]{:S(2)}) copy-start(bf16[512,512]{1,0:T(8,128)(2,1)} %all_gather.22) | copy-start | bytes 1572868
Sparse Core Ops, SparseCore 0:
  11.4 19.4 all-gather.10
  32.5 34.4 all-gather.4
  68.6 94.5 all-gather.8
  164.6 79.8 all-gather.6
